TPU v7x, 32 devices: a whole 2x2x4 slice. The times are simulated.
32 devices in a mesh: dp: 2 (over core), ctx: 4 (over y, x), hd: 4 (over z).
Axes of the slice: x: 2, y: 2, z: 4, core: 2. Of those that a mesh axis runs over, the one named last changes fastest.
Arguments:
- tokens_in: bfloat16 [4, 2048, 1536], P('dp', ('ctx', 'hd')), may hold values from -6 to 6
- seg_ids: int32 [4, 2048], P('dp'), may hold values from 0 to 7, never falling along the last dimension, each value on 1 to 512 neighbouring positions
- in_norm: float32 [1536], replicated, may hold values from 0.5 to 1.5
- z_proj: bfloat16 [1536, 3072], P(('dp', 'ctx', 'hd')), may hold values from -0.15625 to 0.15625
- xbc_proj: bfloat16 [1536, 3328], P(('dp', 'ctx', 'hd')), may hold values from -0.15625 to 0.15625
- dt_proj: bfloat16 [1536, 48], P(('dp', 'ctx', 'hd')), may hold values from -0.0390625 to 0.0390625
- conv_taps: float32 [4, 3328], replicated, may hold values from -3 to 3
- conv_bias: float32 [3328], replicated, may hold values from -2 to 2
- dt_bias: float32 [48], replicated, may hold values from -9 to -2
- a_log: float32 [48], replicated, may hold values from 0 to 2.77
- d_skip: float32 [48], replicated, may hold values from 0.5 to 2
- gate_norm: float32 [3072], replicated, may hold values from 0.5 to 1.5
- out_proj: bfloat16 [3072, 1536], P(('dp', 'ctx', 'hd')), may hold values from -0.109375 to 0.109375
- out_cotangent: bfloat16 [4, 2048, 1536], P('dp', ('ctx', 'hd')), may hold values from -6 to 6
Outputs:
- layer_out: bfloat16 [4, 2048, 1536], P('dp', ('ctx', 'hd'))
- tokens_grad: float32 [4, 2048, 1536], P('dp', ('ctx', 'hd'))
- in_norm_grad: float32 [1536], replicated
- z_proj_grad: float32 [1536, 3072], P(('dp', 'ctx', 'hd'))
- xbc_proj_grad: float32 [1536, 3328], P(('dp', 'ctx', 'hd'))
- dt_proj_grad: float32 [1536, 48], P(('dp', 'ctx', 'hd'))
- conv_taps_grad: float32 [4, 3328], replicated
- conv_bias_grad: float32 [3328], replicated
- dt_bias_grad: float32 [48], replicated
- a_log_grad: float32 [48], replicated
- d_skip_grad: float32 [48], replicated
- gate_norm_grad: float32 [3072], replicated
- out_proj_grad: float32 [3072, 1536], P(('dp', 'ctx', 'hd'))
Inputs may be any that keep to these rules, and one draw needn't show every extreme that they name: `seg_ids`: along each sequence the document numbers never fall; each document has 1 to 512 tokens and one has exactly that many.
All inputs are finite; a program needn't handle non-finite values.
Results may differ from a plain program's by a relative error of at most 0.0097.
Values may be sent and summed in bfloat16 or wider, within the bound.
No kernel may reach another device: no remote copies, remote signals or barrier semaphores. Data moves between devices by JAX's collectives and lax.ppermute only.
A program may use at most 320 MiB of HBM per device.

v0:
```python
import jax
import jax.numpy as jnp
from jax import lax
from jax.sharding import PartitionSpec as P

H = 48
P_SIZE = 64
N = 128
KW = 4
Q = 256
DI = 3072
HIGH = lax.Precision.HIGHEST
EPS = 1e-05


def from_behind(shard, axis, by):
    count = lax.axis_size(axis)
    pairs = [(i, i + by) for i in range(count) if 0 <= i + by < count]
    return lax.ppermute(shard, axis, pairs)


def carried_in(shard, axis, combine, identity, reverse):
    count, place = (lax.axis_size(axis), lax.axis_index(axis))
    everything = jax.tree.map(
        lambda part, kind: lax.all_gather(part.astype(kind), axis),
        shard,
        (jnp.bfloat16, jnp.bfloat16),
    )
    start = jax.tree.map(
        lambda part, zero: jnp.broadcast_to(jnp.asarray(zero, part.dtype), part.shape),
        shard,
        identity,
    )

    def turn(k, before):
        at = count - 1 - k if reverse else k
        reached = at > place if reverse else at < place
        new = combine(
            before, jax.tree.map(lambda part, own: part[at].astype(own.dtype), everything, shard)
        )
        return jax.tree.map(lambda a, b: jnp.where(reached, a, b), new, before)

    return lax.fori_loop(0, count, turn, start)


def norm_rows(values, gain):
    return values * lax.rsqrt(jnp.mean(values * values, axis=-1, keepdims=True) + EPS) * gain


def gate_tail(mixer_val, gate_val, gain):
    return norm_rows(mixer_val * jax.nn.silu(gate_val), gain)


def conv_act(padded, taps, bias, masks):
    length = masks.shape[1]
    mixed = bias
    for tap in range(taps.shape[0]):
        mixed = mixed + taps[tap] * padded[tap : tap + length] * masks[tap][:, None]
    return jax.nn.silu(mixed)


def back_dot(grad_val, weight):
    return lax.dot_general(
        grad_val, weight, (((1,), (1,)), ((), ())), preferred_element_type=jnp.float32
    )


def compose(earlier, later):
    return (earlier[0] * later[0], later[0][:, None, None] * earlier[1] + later[1])


def block_decay(rate_val, bias_here, decay_log, seg_blk, seg_before):
    log_rate = jax.nn.softplus(rate_val + bias_here) * -jnp.exp(decay_log)
    cumul = jnp.cumsum(log_rate, axis=0)
    keep = (seg_blk == seg_before).astype(jnp.float32)
    lead = jnp.exp(cumul) * keep[:, None]
    return (lead[-1], lead)


def block_ssd(
    x_val,
    rate_val,
    bias_here,
    decay_log,
    skip_here,
    bc_val,
    state_in,
    seg_blk,
    seg_before,
    span_len,
):
    length, heads = rate_val.shape
    count = length // span_len
    width_n = bc_val.shape[1] // 2
    x_groups = x_val.reshape(count, span_len, heads, -1)
    dt_groups = jax.nn.softplus(rate_val + bias_here).reshape(count, span_len, heads)
    cumul = jnp.cumsum(dt_groups * -jnp.exp(decay_log), axis=1)
    b_groups = bc_val[:, :width_n].reshape(count, span_len, width_n)
    c_groups = bc_val[:, width_n:].reshape(count, span_len, width_n)
    seg_groups = seg_blk.reshape(count, span_len)
    before = jnp.concatenate([seg_before, seg_groups[:-1, -1]])
    order = jnp.arange(span_len)
    mask = (seg_groups[:, :, None] == seg_groups[:, None, :]) & (order[:, None] >= order[None, :])
    gaps = cumul[:, :, None, :] - cumul[:, None, :, :]
    decay = jnp.exp(jnp.where(mask[..., None], gaps, 0.0)) * mask[..., None].astype(jnp.float32)
    scores = jnp.einsum("ctn,csn->cts", c_groups, b_groups, precision=HIGH)
    mix_w = scores[..., None] * decay * dt_groups[:, None, :, :]
    y_part = jnp.einsum("ctsh,cshp->cthp", mix_w, x_groups, precision=HIGH)
    keep = (seg_groups == before[:, None]).astype(jnp.float32)
    lead = jnp.exp(cumul) * keep[..., None]
    tail = (
        jnp.exp(cumul[:, -1:, :] - cumul)
        * (seg_groups == seg_groups[:, -1:]).astype(jnp.float32)[..., None]
        * dt_groups
    )
    pieces = jnp.einsum("csh,cshp,csn->chpn", tail, x_groups, b_groups, precision=HIGH)

    def advance(state, item):
        piece, factor = item
        return (state * factor[:, None, None] + piece, state)

    state_end, entering = lax.scan(advance, state_in, (pieces, lead[:, -1, :]))
    y_part = y_part + lead[..., None] * jnp.einsum(
        "ctn,chpn->cthp", c_groups, entering, precision=HIGH
    )
    y_part = y_part + skip_here[:, None] * x_groups
    return (y_part.reshape(length, -1), state_end)


def shards(
    tokens_in,
    seg_ids,
    in_norm,
    z_proj,
    xbc_proj,
    dt_proj,
    conv_taps,
    conv_bias,
    dt_bias,
    a_log,
    d_skip,
    gate_norm,
    out_proj,
    out_cotangent,
):
    batches, rows, width = tokens_in.shape
    n_heads_axis = lax.axis_size("hd")
    heads_here = H // n_heads_axis
    block = rows * n_heads_axis
    channels = DI + 2 * N
    start_tok = lax.axis_index(("ctx", "hd")) * rows
    start_blk = lax.axis_index("ctx") * block
    head_low = lax.axis_index("hd") * heads_here
    bias_here = lax.dynamic_slice_in_dim(dt_bias, head_low, heads_here)
    decay_log = lax.dynamic_slice_in_dim(a_log, head_low, heads_here)
    skip_here = lax.dynamic_slice_in_dim(d_skip, head_low, heads_here)
    unit = (jnp.ones((heads_here,), jnp.float32), jnp.zeros((heads_here, P_SIZE, N), jnp.float32))

    def fetch():
        return (
            lax.all_gather(z_proj, ("dp", "ctx", "hd"), axis=0, tiled=True),
            lax.all_gather(xbc_proj, ("dp", "ctx", "hd"), axis=0, tiled=True),
            lax.all_gather(dt_proj, ("dp", "ctx", "hd"), axis=0, tiled=True),
            lax.all_gather(out_proj, ("dp", "ctx", "hd"), axis=0, tiled=True),
        )

    stored = []
    outputs = []
    for batch in range(batches):
        zed_weight, xbc_weight, rate_weight, out_weight = fetch()
        seg_row = seg_ids[batch]
        seg_pad = jnp.concatenate([jnp.full((KW - 1,), -1, jnp.int32), seg_row])
        seg_near = lax.dynamic_slice_in_dim(seg_pad, start_tok, rows + KW - 1)
        seg_own = seg_near[KW - 1 :]
        masks = jnp.stack([seg_near[tap : tap + rows] == seg_own for tap in range(KW)]).astype(
            jnp.float32
        )
        seg_blk = lax.dynamic_slice_in_dim(seg_row, start_blk, block)
        seg_before = lax.dynamic_slice_in_dim(seg_pad, start_blk + KW - 2, 1)
        source = tokens_in[batch].astype(jnp.float32)
        normed = norm_rows(source, in_norm).astype(jnp.bfloat16)
        gate_in = jnp.dot(normed, zed_weight, preferred_element_type=jnp.float32)
        raw_xbc = jnp.dot(normed, xbc_weight, preferred_element_type=jnp.float32).astype(
            jnp.bfloat16
        )
        rate_raw = jnp.dot(normed, rate_weight, preferred_element_type=jnp.float32).astype(
            jnp.bfloat16
        )
        rim_rows = from_behind(raw_xbc[rows - (KW - 1) :], ("ctx", "hd"), 1)
        padded = jnp.concatenate([rim_rows, raw_xbc], 0).astype(jnp.float32)
        active = conv_act(padded, conv_taps, conv_bias, masks)
        x_low = active[:, :DI].astype(jnp.bfloat16)
        bc_low = active[:, DI:].astype(jnp.bfloat16)
        x_heads, rate_heads = (
            lax.all_to_all(x_low, "hd", split_axis=1, concat_axis=0, tiled=True),
            lax.all_to_all(rate_raw, "hd", split_axis=1, concat_axis=0, tiled=True),
        )
        bc_all = lax.all_gather(bc_low, "hd", axis=0, tiled=True)
        x_float = x_heads.astype(jnp.float32)
        rate_float = rate_heads.astype(jnp.float32)
        bc_float = bc_all.astype(jnp.float32)
        zero_state = jnp.zeros((heads_here, P_SIZE, N), jnp.float32)
        y_zero, state_local = block_ssd(
            x_float,
            rate_float,
            bias_here,
            decay_log,
            skip_here,
            bc_float,
            zero_state,
            seg_blk,
            seg_before,
            Q,
        )
        total_decay, lead_blk = block_decay(rate_float, bias_here, decay_log, seg_blk, seg_before)
        unused, state_in = carried_in((total_decay, state_local), "ctx", compose, unit, False)
        carried = lead_blk[:, :, None] * jnp.einsum(
            "tn,hpn->thp", bc_float[:, N:], state_in, precision=HIGH
        )
        y_heads = y_zero + carried.reshape(block, -1)
        y_tokens = lax.all_to_all(
            y_heads.astype(jnp.bfloat16), "hd", split_axis=0, concat_axis=1, tiled=True
        )
        y_float = y_tokens.astype(jnp.float32)
        gated = gate_tail(y_float, gate_in, gate_norm).astype(jnp.bfloat16)
        result = source + jnp.dot(gated, out_weight, preferred_element_type=jnp.float32)
        outputs.append(result.astype(jnp.bfloat16))
        stored.append(
            (
                source,
                normed,
                gate_in,
                padded,
                masks,
                x_float,
                rate_float,
                bc_float,
                seg_blk,
                seg_before,
                lead_blk,
                total_decay,
                state_in,
                y_float,
                gated,
            )
        )
    grads_tok = []
    normed_rows = []
    proj_grads = []
    gated_rows = []
    cot_rows = []
    norm_total = jnp.zeros((width,), jnp.float32)
    taps_total = jnp.zeros(conv_taps.shape, jnp.float32)
    cbias_total = jnp.zeros((channels,), jnp.float32)
    dtb_total = jnp.zeros((H,), jnp.float32)
    alog_total = jnp.zeros((H,), jnp.float32)
    skip_total = jnp.zeros((H,), jnp.float32)
    gate_total = jnp.zeros((DI,), jnp.float32)
    for batch in range(batches):
        zed_weight, xbc_weight, rate_weight, out_weight = fetch()
        (
            source,
            normed,
            gate_in,
            padded,
            masks,
            x_float,
            rate_float,
            bc_float,
            seg_blk,
            seg_before,
            lead_blk,
            total_decay,
            state_in,
            y_float,
            gated,
        ) = stored[batch]
        cot_low = out_cotangent[batch]
        d_gated = back_dot(cot_low, out_weight)
        unused, tail_pull = jax.vjp(gate_tail, y_float, gate_in, gate_norm)
        d_mixer, d_gate_in, d_gain = tail_pull(d_gated)
        d_mixer_heads = lax.all_to_all(
            d_mixer.astype(jnp.bfloat16), "hd", split_axis=1, concat_axis=0, tiled=True
        )
        d_y_float = d_mixer_heads.astype(jnp.float32)
        d_local = jnp.einsum(
            "th,thp,tn->hpn",
            lead_blk,
            d_y_float.reshape(block, heads_here, P_SIZE),
            bc_float[:, N:],
            precision=HIGH,
        )
        unused, d_end = carried_in((total_decay, d_local), "ctx", compose, unit, True)

        def with_state(x_value, rate_value, bias_value, decay_value, skip_value, bc_value):
            return block_ssd(
                x_value,
                rate_value,
                bias_value,
                decay_value,
                skip_value,
                bc_value,
                state_in,
                seg_blk,
                seg_before,
                Q,
            )

        unused, ssd_pull = jax.vjp(
            with_state, x_float, rate_float, bias_here, decay_log, skip_here, bc_float
        )
        d_x_heads, d_rate_heads, d_bias_h, d_decay_h, d_skip_h, d_bc_heads = ssd_pull(
            (d_y_float, d_end)
        )
        d_x_tok, d_rate_tok = (
            lax.all_to_all(
                d_x_heads.astype(jnp.bfloat16), "hd", split_axis=0, concat_axis=1, tiled=True
            ),
            lax.all_to_all(
                d_rate_heads.astype(jnp.bfloat16), "hd", split_axis=0, concat_axis=1, tiled=True
            ),
        )
        d_bc_tok = lax.psum_scatter(
            d_bc_heads.astype(jnp.bfloat16), "hd", scatter_dimension=0, tiled=True
        ).astype(jnp.float32)
        d_active = jnp.concatenate([d_x_tok.astype(jnp.float32), d_bc_tok], axis=1)

        def conv_here(pad_value, taps_value, bias_value):
            return conv_act(pad_value, taps_value, bias_value, masks)

        unused, conv_pull = jax.vjp(conv_here, padded, conv_taps, conv_bias)
        d_padded, d_taps, d_cbias = conv_pull(d_active)
        back_rim = from_behind(d_padded[: KW - 1].astype(jnp.bfloat16), ("ctx", "hd"), -1).astype(
            jnp.float32
        )
        d_raw = d_padded[KW - 1 :] + jnp.concatenate(
            [jnp.zeros((rows - (KW - 1), channels), jnp.float32), back_rim], 0
        )
        d_raw_low = d_raw.astype(jnp.bfloat16)
        d_gate_low = d_gate_in.astype(jnp.bfloat16)
        d_normed = (
            back_dot(d_gate_low, zed_weight)
            + back_dot(d_raw_low, xbc_weight)
            + back_dot(d_rate_tok, rate_weight)
        )
        unused, norm_pull = jax.vjp(norm_rows, source, in_norm)
        d_source, d_norm_gain = norm_pull(d_normed)
        grads_tok.append(d_source + cot_low.astype(jnp.float32))
        normed_rows.append(normed)
        proj_grads.append(jnp.concatenate([d_gate_low, d_raw_low, d_rate_tok], axis=1))
        gated_rows.append(gated)
        cot_rows.append(cot_low)
        norm_total = norm_total + d_norm_gain
        taps_total = taps_total + d_taps
        cbias_total = cbias_total + d_cbias
        dtb_total = dtb_total + lax.dynamic_update_slice_in_dim(
            jnp.zeros((H,), jnp.float32), d_bias_h, head_low, 0
        )
        alog_total = alog_total + lax.dynamic_update_slice_in_dim(
            jnp.zeros((H,), jnp.float32), d_decay_h, head_low, 0
        )
        skip_total = skip_total + lax.dynamic_update_slice_in_dim(
            jnp.zeros((H,), jnp.float32), d_skip_h, head_low, 0
        )
        gate_total = gate_total + d_gain
    normed_all = jnp.concatenate(normed_rows, 0)
    proj_all = jnp.concatenate(proj_grads, 0)
    gated_all = jnp.concatenate(gated_rows, 0)
    cot_all = jnp.concatenate(cot_rows, 0)
    part = normed_all
    in_grad = lax.psum_scatter(
        lax.dot_general(
            part, proj_all, (((0,), (0,)), ((), ())), preferred_element_type=jnp.float32
        ),
        ("dp", "ctx", "hd"),
        scatter_dimension=0,
        tiled=True,
    )
    part = gated_all
    out_grad = lax.psum_scatter(
        lax.dot_general(
            part, cot_all, (((0,), (0,)), ((), ())), preferred_element_type=jnp.float32
        ),
        ("dp", "ctx", "hd"),
        scatter_dimension=0,
        tiled=True,
    )
    norm_sum, taps_sum, cbias_sum, dtb_sum, alog_sum, skip_sum, gate_sum = lax.psum(
        (norm_total, taps_total, cbias_total, dtb_total, alog_total, skip_total, gate_total),
        ("dp", "ctx", "hd"),
    )
    return (
        jnp.stack(outputs),
        jnp.stack(grads_tok),
        norm_sum,
        in_grad[:, :DI],
        in_grad[:, DI : DI + channels],
        in_grad[:, DI + channels :],
        taps_sum,
        cbias_sum,
        dtb_sum,
        alog_sum,
        skip_sum,
        gate_sum,
        out_grad,
    )


def solution(mesh):
    in_specs = (
        P("dp", ("ctx", "hd"), None),
        P("dp", None),
        P(),
        P(("dp", "ctx", "hd"), None),
        P(("dp", "ctx", "hd"), None),
        P(("dp", "ctx", "hd"), None),
        P(),
        P(),
        P(),
        P(),
        P(),
        P(),
        P(("dp", "ctx", "hd"), None),
        P("dp", ("ctx", "hd"), None),
    )
    out_specs = (
        P("dp", ("ctx", "hd"), None),
        P("dp", ("ctx", "hd"), None),
        P(),
        P(("dp", "ctx", "hd"), None),
        P(("dp", "ctx", "hd"), None),
        P(("dp", "ctx", "hd"), None),
        P(),
        P(),
        P(),
        P(),
        P(),
        P(),
        P(("dp", "ctx", "hd"), None),
    )
    return jax.shard_map(shards, mesh=mesh, in_specs=in_specs, out_specs=out_specs, check_vma=False)
```

profile of v0, /device:TPU:0, one launch (start us, length us, event | category | flops | bytes accessed | tf_op | source)
XLA Modules:
  0.0 1491.1 jit_solution(12795185626710274791)
XLA Ops:
  8.7 76.8 %all_gather.68 = bf16[1536,48]{1,0:T(8,128)(2,1)S(1)} all-gather(bf16[48,48]{1,0:T(8,128)(2,1)} %param.40), channel_id=1, replica_groups=mesh['dp'=2,'ctx'=4,'hd'=4] {'dp','ctx','hd'}, dimensions={0}, use_global_device_ids=true | all-gather | bytes 152064 | tf_op jit(solution)/shard_map/all_gather | solution.py:163
  105.2 5.0 all-to-all-start.1
  110.2 5.7 all-to-all-done.1
  125.4 14.0 all-gather.5
  141.8 6.4 all-gather.4
  152.6 6.6 convolution_convert_fusion
  173.7 6.7 all-to-all-start.3
  188.7 17.7 %all_gather.74 = bf16[512,256]{1,0:T(8,128)(2,1)S(1)} all-gather(bf16[128,256]{1,0:T(8,128)(2,1)S(1)} %slice.403), channel_id=1, replica_groups=mesh['dp'=2,'ctx'=4,'hd'=4] {'hd'}, dimensions={0}, use_global_device_ids=true | all-gather | bytes 327680 | tf_op jit(solution)/shard_map/all_gather | solution.py:198
  206.4 15.0 %all_gather.33 = bf16[512,256]{1,0:T(8,128)(2,1)S(1)} all-gather(bf16[128,256]{1,0:T(8,128)(2,1)S(1)} %slice.386), channel_id=1, replica_groups=mesh['dp'=2,'ctx'=4,'hd'=4] {'hd'}, dimensions={0}, use_global_device_ids=true | all-gather | bytes 327680 | tf_op jit(solution)/shard_map/all_gather | solution.py:198
  224.1 4.6 all-to-all-start
  238.3 7.7 while.156
  247.1 12.9 all-gather.1
  260.0 6.8 while.157
  269.1 5.0 fusion.103
  289.1 14.6 all-to-all-start.5
  313.3 7.6 while.154
  321.9 11.6 all-gather
  336.4 6.8 while.155
  343.1 7.1 fusion.101
  352.7 3.6 reshape.741
  369.2 5.5 all-to-all-start.2
  376.4 6.3 while.152
  393.6 7.3 multiply_reduce_fusion.19
  401.5 9.2 multiply_reduce_fusion.13
  410.8 7.1 multiply_reduce_fusion.18
  418.0 9.1 multiply_convert_fusion.3
  427.1 4.9 multiply_convert_fusion.2
  434.2 5.1 all-to-all-start.9
  440.3 3.9 while.150
  446.5 13.0 all-to-all-done.9
  459.5 4.2 all-to-all-start.6
  472.3 10.0 all-gather.3
  495.6 7.8 while.153
  509.5 6.3 fusion.53
  524.5 12.2 all-gather.2
  536.7 4.4 while.158
  553.0 6.8 while.151
  565.2 6.4 fusion.51
  580.1 6.3 reduce-window.70
  603.2 6.2 reduce-window.76
  620.8 5.0 all-to-all-start.11
  628.5 4.3 all-to-all-done.11
  632.9 4.3 all-to-all-start.8
  637.2 6.4 fusion.116
  648.0 5.1 all-to-all-start.10
  653.0 6.3 fusion.109
  666.6 3.9 fusion.144
  675.4 5.2 all-to-all-start.7
  683.9 4.0 fusion.145
  699.4 4.7 reduce-scatter.7.cloned.1.call-done
  704.1 4.1 multiply_reduce_fusion.5
  708.2 16.6 %reduce-scatter.5.cloned.1.call-done = bf16[128,256]{1,0:T(8,128)(2,1)} async-done(((bf16[512,256]{1,0:T(8,128)(2,1)}), bf16[128,256]{1,0:T(8,128)(2,1)}) %reduce-scatter.5.cloned.1.call-update) | async-done | bytes 65552 | tf_op jit(solution)/shard_map/reduce_scatter | solution.py:323
  724.8 6.5 multiply_reduce_fusion.9
  741.9 19.9 %fusion.38 = f32[1536,6448]{1,0:T(8,128)} fusion(bf16[128,48]{1,0:T(8,128)(2,1)S(1)} %copy.500, bf16[128,3328]{1,0:T(8,128)(2,1)S(1)} %fusion.98, bf16[128,3072]{1,0:T(8,128)(2,1)S(1)} %copy-done.28, bf16[128,48]{1,0:T(8,128)(2,1)S(1)} %copy-done.103, bf16[128,3328]{1,0:T(8,128)(2,1)S(1)} %fusion.99, bf16[128,3072]{1,0:T(8,128)(2,1)} %get-tuple-element.1175, ...), kind=kOutput, calls=%fused_computation.78 | convolution fusion | flops 5092294656 | bytes 43704320 | tf_op jit(solution)/shard_map/dot_general | solution.py:372
  764.4 7.0 fusion.278
  771.4 9.5 fusion.276
  788.5 8.9 convolution_add_fusion.2
  798.7 9.0 convolution_add_fusion.3
  809.9 11.9 fusion.118
  821.8 6.1 fusion.84
  828.0 5.1 fusion.85
  836.5 293.6 %reduce-scatter.9.cloned.1.call-done = f32[48,6448]{1,0:T(8,128)} async-done(((f32[1536,6448]{1,0:T(8,128)}), f32[48,6448]{1,0:T(8,128)}) %reduce-scatter.9.cloned.1.call-update) | async-done | bytes 1238032 | tf_op jit(solution)/shard_map/reduce_scatter | solution.py:371
  1135.3 125.0 %all-reduce.31.cloned.1.call-done = (f32[1536]{0:T(1024)}, f32[4,3328]{1,0:T(4,128)}, f32[3328]{0:T(1024)}, f32[48]{0:T(128)}, f32[48]{0:T(128)}, /*index=5*/f32[48]{0:T(128)}, f32[3072]{0:T(1024)}) async-done(((f32[1536]{0:T(1024)}, f32[4,3328]{1,0:T(4,128)}, f32[3328]{0:T(1024)}, f32[48]{0:T(128)}, f32[48]{0:T(128)}, /*index=5*/f32[48]{0:T(128)}, f32[3072]{0:T(1024)}), (f32[1536]{0:T(1024)}, ...) | async-done | bytes 85584 | tf_op jit(solution)/shard_map/psum | solution.py:388
  1260.2 214.8 %reduce-scatter.11.cloned.1.call-done = f32[96,1536]{1,0:T(8,128)} async-done(((f32[3072,1536]{1,0:T(8,128)}), f32[96,1536]{1,0:T(8,128)}) %reduce-scatter.11.cloned.1.call-update) | async-done | bytes 589840 | tf_op jit(solution)/shard_map/reduce_scatter | solution.py:380
  (814 shorter events, 362.9 us)
Async XLA Ops:
  7.2 80.4 %copy-start.12 = (bf16[2,128,1536]{2,1,0:T(8,128)(2,1)S(1)}, bf16[2,128,1536]{2,1,0:T(8,128)(2,1)}, u32[]{:S(2)}) copy-start(bf16[2,128,1536]{2,1,0:T(8,128)(2,1)} %param.35) | copy-start | bytes 2359300
  7.2 80.4 %copy-start.127 = (f32[1536]{0:T(1024)S(1)}, f32[1536]{0:T(1024)}, u32[]{:S(2)}) copy-start(f32[1536]{0:T(1024)} %param.37) | copy-start | bytes 18436
  7.2 145.4 %all-gather.10.cloned.1.call-start = ((), (), s32[]{:S(2)}) async-start(), calls=%async_computation.16 | async-start | bytes 10543104 | tf_op jit(solution)/shard_map/all_gather | solution.py:162
  7.9 385.7 %all-gather.12.cloned.1.call-start = ((), (), s32[]{:S(2)}) async-start(), calls=%async_computation.17 | async-start | bytes 9732096 | tf_op jit(solution)/shard_map/all_gather | solution.py:161
  85.5 11.8 copy-start.33
  85.5 11.1 copy-start.120
  87.1 10.5 copy-start.158
  87.1 10.5 copy-start.160
  87.8 64.8 %copy-start.18 = (bf16[128,1536]{1,0:T(8,128)(2,1)}, bf16[128,1536]{1,0:T(8,128)(2,1)S(1)}, u32[]{:S(2)}) copy-start(bf16[128,1536]{1,0:T(8,128)(2,1)S(1)} %get-tuple-element.1191) | copy-start | bytes 1179652
  87.8 74.5 %copy-start.15 = (bf16[128,1536]{1,0:T(8,128)(2,1)}, bf16[128,1536]{1,0:T(8,128)(2,1)S(1)}, u32[]{:S(2)}) copy-start(bf16[128,1536]{1,0:T(8,128)(2,1)S(1)} %get-tuple-element.1190) | copy-start | bytes 1179652
  87.9 15.9 %copy-start.172 = (f32[48]{0:T(128)S(1)}, f32[48]{0:T(128)}, u32[]{:S(2)}) copy-start(f32[48]{0:T(128)} %param.44) | copy-start | bytes 580
  87.9 16.0 %copy-start.178 = (f32[48]{0:T(128)S(1)}, f32[48]{0:T(128)}, u32[]{:S(2)}) copy-start(f32[48]{0:T(128)} %param.43) | copy-start | bytes 580
  88.2 16.4 %copy-start.179 = (f32[48]{0:T(128)S(1)}, f32[48]{0:T(128)}, u32[]{:S(2)}) copy-start(f32[48]{0:T(128)} %param.45) | copy-start | bytes 580
  88.8 16.4 %all-to-all-start.4 = ((bf16[128,4,12]{0,2,1:T(8,128)(2,1)}), bf16[128,4,12]{0,2,1:T(8,128)(2,1)S(1)}, u32[]{:S(2)}, u32[]{:S(2)}) async-start(bf16[128,4,12]{0,2,1:T(8,128)(2,1)} %all_to_all.141), calls=%async_computation.4 | async-start | bytes 32768 | tf_op jit(solution)/shard_map/all_to_all | solution.py:196
  92.1 309.4 %all-gather.14.cloned.1.call-start = ((), (), s32[]{:S(2)}) async-start(), calls=%async_computation.18 | async-start | bytes 9732096 | tf_op jit(solution)/shard_map/all_gather | solution.py:164
  97.3 84.5 %copy-start.80 = (f32[3328]{0:T(1024)}, f32[3328]{0:T(1024)S(1)}, u32[]{:S(2)}) copy-start(f32[3328]{0:T(1024)S(1)} %get-tuple-element.1033) | copy-start | bytes 39940
  101.0 47.9 %copy-start.121 = (f32[2,256]{1,0:T(2,128)}, f32[2,256]{1,0:T(2,128)S(1)}, u32[]{:S(2)}) copy-start(f32[2,256]{1,0:T(2,128)S(1)} %get-tuple-element.1240) | copy-start | bytes 6148
  101.0 47.9 %copy-start.137 = (f32[2,256]{1,0:T(2,128)}, f32[2,256]{1,0:T(2,128)S(1)}, u32[]{:S(2)}) copy-start(f32[2,256]{1,0:T(2,128)S(1)} %get-tuple-element.1241) | copy-start | bytes 6148
  102.4 46.4 %copy-start.136 = (f32[2,256]{1,0:T(2,128)}, f32[2,256]{1,0:T(2,128)S(1)}, u32[]{:S(2)}) copy-start(f32[2,256]{1,0:T(2,128)S(1)} %get-tuple-element.1247) | copy-start | bytes 6148
  103.8 16.4 %copy-start.156 = (f32[12]{0:T(128)}, f32[12]{0:T(128)S(1)}, u32[]{:S(2)}) copy-start(f32[12]{0:T(128)S(1)} %fusion.252) | copy-start | bytes 148
  104.0 44.9 %copy-start.157 = (f32[12]{0:T(128)}, f32[12]{0:T(128)S(1)}, u32[]{:S(2)}) copy-start(f32[12]{0:T(128)S(1)} %dynamic_slice.178) | copy-start | bytes 148
  105.2 10.8 all-to-all-start.1
  116.1 25.5 %copy-start.78 = (f32[2,8,4,128]{3,1,2,0:T(8,128)}, f32[2,8,4,128]{3,1,2,0:T(8,128)S(1)}, u32[]{:S(2)}) copy-start(f32[2,8,4,128]{3,1,2,0:T(8,128)S(1)} %copy.565) | copy-start | bytes 98308
  116.1 25.5 %copy-start.79 = (f32[2,8,4,128]{3,1,2,0:T(8,128)}, f32[2,8,4,128]{3,1,2,0:T(8,128)S(1)}, u32[]{:S(2)}) copy-start(f32[2,8,4,128]{3,1,2,0:T(8,128)S(1)} %copy.563) | copy-start | bytes 98308
  116.2 33.4 %copy-start.63 = (f32[2,256,12]{1,0,2:T(2,128)}, f32[2,256,12]{1,0,2:T(2,128)S(1)}, u32[]{:S(2)}) copy-start(f32[2,256,12]{1,0,2:T(2,128)S(1)} %reshape.754) | copy-start | bytes 73732
  116.3 33.4 %copy-start.61 = (f32[2,256,12]{1,0,2:T(2,128)}, f32[2,256,12]{1,0,2:T(2,128)S(1)}, u32[]{:S(2)}) copy-start(f32[2,256,12]{1,0,2:T(2,128)S(1)} %reshape.763) | copy-start | bytes 73732
  118.6 40.6 %copy-start.93 = (f32[2,12,256]{2,1,0:T(8,128)}, f32[2,12,256]{2,1,0:T(8,128)S(1)}, u32[]{:S(2)}) copy-start(f32[2,12,256]{2,1,0:T(8,128)S(1)} %reshape.833) | copy-start | bytes 73732
  120.4 38.8 %copy-start.134 = (f32[2,12]{1,0:T(2,128)}, f32[2,12]{1,0:T(2,128)S(1)}, u32[]{:S(2)}) copy-start(f32[2,12]{1,0:T(2,128)S(1)} %slice_reduce_fusion.10) | copy-start | bytes 292
  122.0 37.3 %copy-start.59 = (f32[2,12,256]{2,1,0:T(8,128)}, f32[2,12,256]{2,1,0:T(8,128)S(1)}, u32[]{:S(2)}) copy-start(f32[2,12,256]{2,1,0:T(8,128)S(1)} %reshape.841) | copy-start | bytes 73732
  122.1 37.1 %copy-start.132 = (f32[2,12]{1,0:T(2,128)}, f32[2,12]{1,0:T(2,128)S(1)}, u32[]{:S(2)}) copy-start(f32[2,12]{1,0:T(2,128)S(1)} %slice_reduce_fusion.8) | copy-start | bytes 292
  123.7 35.6 %copy-start.94 = (f32[2,12,256]{2,1,0:T(8,128)}, f32[2,12,256]{2,1,0:T(8,128)S(1)}, u32[]{:S(2)}) copy-start(f32[2,12,256]{2,1,0:T(8,128)S(1)} %reshape.835) | copy-start | bytes 73732
  125.2 16.3 %copy-start.76 = (f32[512,12]{0,1:T(8,128)}, f32[512,12]{0,1:T(8,128)S(1)}, u32[]{:S(2)}) copy-start(f32[512,12]{0,1:T(8,128)S(1)} %multiply_bitcast_fusion.2) | copy-start | bytes 73732
  141.6 17.7 %copy-start.74 = (f32[512,12]{0,1:T(8,128)}, f32[512,12]{0,1:T(8,128)S(1)}, u32[]{:S(2)}) copy-start(f32[512,12]{0,1:T(8,128)S(1)} %multiply_bitcast_fusion.5) | copy-start | bytes 73732
  159.3 7.4 collective-permute-start.1
  164.6 15.9 %collective-permute-start = (bf16[3,3328]{1,0:T(4,128)(2,1)}, bf16[3,3328]{1,0:T(4,128)(2,1)S(1)}, u32[]{:S(2)}, u32[]{:S(2)}) collective-permute-start(bf16[3,3328]{1,0:T(4,128)(2,1)} %slice.380), channel_id=1, source_target_pairs={{0,1},{1,2},{2,3},{3,4},{4,5},{5,6},{6,7},{7,8},{8,9},{9,10},{10,1... | collective-permute-start | bytes 59912 | tf_op jit(solution)/shard_map/ppermute | solution.py:19
  173.7 50.4 %all-to-all-start.3 = ((bf16[128,4,768]{0,2,1:T(8,128)(2,1)}), bf16[128,4,768]{0,2,1:T(8,128)(2,1)}, u32[]{:S(2)}, u32[]{:S(2)}) async-start(bf16[128,4,768]{0,2,1:T(8,128)(2,1)} %bitcast.581), calls=%async_computation.3 | async-start | bytes 1572864 | tf_op jit(solution)/shard_map/all_to_all | solution.py:195
  206.4 16.7 %copy-start.54 = (bf16[512,256]{1,0:T(8,128)(2,1)}, bf16[512,256]{1,0:T(8,128)(2,1)S(1)}, u32[]{:S(2)}) copy-start(bf16[512,256]{1,0:T(8,128)(2,1)S(1)} %all_gather.74) | copy-start | bytes 786436
  224.1 64.9 %all-to-all-start = ((bf16[128,4,768]{0,2,1:T(8,128)(2,1)}), bf16[128,4,768]{0,2,1:T(8,128)(2,1)}, u32[]{:S(2)}, u32[]{:S(2)}) async-start(bf16[128,4,768]{0,2,1:T(8,128)(2,1)} %bitcast.579), calls=%async_computation | async-start | bytes 1572864 | tf_op jit(solution)/shard_map/all_to_all | solution.py:195
  289.1 80.1 %all-to-all-start.5 = ((bf16[4,128,768]{1,2,0:T(8,128)(2,1)}), bf16[4,128,768]{1,2,0:T(8,128)(2,1)}, u32[]{:S(2)}, u32[]{:S(2)}) async-start(bf16[4,128,768]{1,2,0:T(8,128)(2,1)} %copy.441), calls=%async_computation.5 | async-start | bytes 1572864 | tf_op jit(solution)/shard_map/all_to_all | solution.py:221
  320.8 12.7 copy-start.49
  369.2 18.9 %all-to-all-start.2 = ((bf16[4,128,768]{1,2,0:T(8,128)(2,1)}), bf16[4,128,768]{1,2,0:T(8,128)(2,1)}, u32[]{:S(2)}, u32[]{:S(2)}) async-start(bf16[4,128,768]{1,2,0:T(8,128)(2,1)} %copy.425), calls=%async_computation.2 | async-start | bytes 1572864 | tf_op jit(solution)/shard_map/all_to_all | solution.py:221
  401.5 16.5 %slice-start = ((s8[9437184]{0:T(1024)(128)(4,1)}), s8[4194304]{0:T(1024)(128)(4,1)S(1)}, s32[]{:S(2)}) async-start(s8[9437184]{0:T(1024)(128)(4,1)} %bitcast.551), calls=%async_computation.24 | async-start | bytes 8388608
  401.5 16.5 %slice-start.1 = ((s8[9437184]{0:T(1024)(128)(4,1)}), s8[4194304]{0:T(1024)(128)(4,1)S(1)}, s32[]{:S(2)}) async-start(s8[9437184]{0:T(1024)(128)(4,1)} %bitcast.551), calls=%async_computation.25 | async-start | bytes 8388608
  434.2 25.3 %all-to-all-start.9 = ((bf16[128,4,768]{0,2,1:T(8,128)(2,1)}), bf16[128,4,768]{0,2,1:T(8,128)(2,1)}, u32[]{:S(2)}, u32[]{:S(2)}) async-start(bf16[128,4,768]{0,2,1:T(8,128)(2,1)} %bitcast.580), calls=%async_computation.10 | async-start | bytes 1572864 | tf_op jit(solution)/shard_map/all_to_all | solution.py:282
  444.2 20.7 %copy-start.180 = (f32[2,12,1,1]{1,3,2,0:T(1,128)}, f32[2,12,1,1]{1,3,2,0:T(1,128)S(1)}, u32[]{:S(2)}) copy-start(f32[2,12,1,1]{1,3,2,0:T(1,128)S(1)} %get-tuple-element.1855) | copy-start | bytes 292
  459.5 56.3 %all-to-all-start.6 = ((bf16[128,4,768]{0,2,1:T(8,128)(2,1)}), bf16[128,4,768]{0,2,1:T(8,128)(2,1)}, u32[]{:S(2)}, u32[]{:S(2)}) async-start(bf16[128,4,768]{0,2,1:T(8,128)(2,1)} %bitcast.84), calls=%async_computation.6 | async-start | bytes 1572864 | tf_op jit(solution)/shard_map/all_to_all | solution.py:282
  522.2 14.5 copy-start.174
  571.6 65.6 %copy-start.22 = (bf16[2,256,12,64]{1,0,3,2:T(2,128)(2,1)S(1)}, bf16[2,256,12,64]{1,0,3,2:T(2,128)(2,1)}, u32[]{:S(2)}) copy-start(bf16[2,256,12,64]{1,0,3,2:T(2,128)(2,1)} %all_to_all.156) | copy-start | bytes 2359300
  620.8 12.0 all-to-all-start.11
  632.9 15.1 %all-to-all-start.8 = ((bf16[4,128,12]{1,2,0:T(8,128)(2,1)}), bf16[4,128,12]{1,2,0:T(8,128)(2,1)}, u32[]{:S(2)}, u32[]{:S(2)}) async-start(bf16[4,128,12]{1,2,0:T(8,128)(2,1)} %copy.470), calls=%async_computation.9 | async-start | bytes 32768 | tf_op jit(solution)/shard_map/all_to_all | solution.py:319
  648.0 27.4 %all-to-all-start.10 = ((bf16[4,128,768]{1,2,0:T(8,128)(2,1)}), bf16[4,128,768]{1,2,0:T(8,128)(2,1)}, u32[]{:S(2)}, u32[]{:S(2)}) async-start(bf16[4,128,768]{1,2,0:T(8,128)(2,1)} %copy.484), calls=%async_computation.11 | async-start | bytes 1572864 | tf_op jit(solution)/shard_map/all_to_all | solution.py:316
  675.4 21.7 %all-to-all-start.7 = ((bf16[4,128,768]{1,2,0:T(8,128)(2,1)}), bf16[4,128,768]{1,2,0:T(8,128)(2,1)}, u32[]{:S(2)}, u32[]{:S(2)}) async-start(bf16[4,128,768]{1,2,0:T(8,128)(2,1)} %copy.456), calls=%async_computation.7 | async-start | bytes 1572864 | tf_op jit(solution)/shard_map/all_to_all | solution.py:316
  680.6 23.5 %reduce-scatter.7.cloned.1.call-start = ((), (), s32[]{:S(2)}) async-start(), calls=%async_computation.20 | async-start | bytes 327680 | tf_op jit(solution)/shard_map/reduce_scatter | solution.py:323
  683.6 41.1 %reduce-scatter.5.cloned.1.call-start = ((), (), s32[]{:S(2)}) async-start(), calls=%async_computation.19 | async-start | bytes 327680 | tf_op jit(solution)/shard_map/reduce_scatter | solution.py:323
  692.4 11.7 copy-start.141
  692.4 11.6 copy-start.143
  692.4 437.6 %reduce-scatter.9.cloned.1.call-start = ((), (), s32[]{:S(2)}) async-start(), calls=%async_computation.21 | async-start | bytes 41361408 | tf_op jit(solution)/shard_map/reduce_scatter | solution.py:371
  693.2 10.8 copy-start.104
  733.4 5.8 collective-permute-start.3
  735.3 6.4 collective-permute-start.2
  761.8 498.5 %all-reduce.31.cloned.1.call-start = ((), (), s32[]{:S(2)}) async-start(), calls=%async_computation.23 | async-start | bytes 183296 | tf_op jit(solution)/shard_map/psum | solution.py:388
  786.1 11.3 copy-start.170
  786.5 10.9 copy-start.163
  809.9 665.2 %reduce-scatter.11.cloned.1.call-start = ((), (), s32[]{:S(2)}) async-start(), calls=%async_computation.22 | async-start | bytes 19464192 | tf_op jit(solution)/shard_map/reduce_scatter | solution.py:380
  (150 other events, 703.8 us)
Sparse Core Ops, SparseCore 0:
  10.8 90.7 all-gather.9
  104.4 90.3 all-gather.11
  197.6 94.1 all-gather.13
  683.9 20.1 reduce-scatter.6
  706.8 17.8 reduce-scatter.4
  761.9 368.0 reduce-scatter.8
  1137.6 122.5 all-reduce.30
  1267.2 207.8 reduce-scatter.10
where the time goes:
time: 1500 us; the launch traced here: 1490 us
  waiting for transfers between devices  684 us (46%)
  matrix products  216 us (14%)
  local copies, waits for them, and re-layouts  179 us (12%)
  blocking collectives  177 us (12%)
  other arithmetic  140 us (9%)
  starting transfers between devices  77 us (5%)
  between operations  17.4 us (1%)
    reduce_scatter x1, waiting for transfers between devices, shards(): lax.psum_scatter(lax.dot_general(part, proj_all, (((0,), (0,)), ((), ()))...  294 us
    reduce_scatter x1, waiting for transfers between devices, shards(): lax.psum_scatter(lax.dot_general(part, cot_all, (((0,), (0,)), ((), ())),...  215 us
    psum x1, waiting for transfers between devices, shards(): lax.psum((norm_total, taps_total, cbias_total, dtb_total, alog_total, ski...  125 us
    all_gather x1, blocking collectives, fetch(): lax.all_gather(dt_proj, ('dp', 'ctx', 'hd'), axis=0, tiled=True)  76.8 us
    all_gather x6, blocking collectives, carried_in(): lax.all_gather(part.astype(kind), axis)  67.1 us
    dot_general x8, matrix products, back_dot(): lax.dot_general(grad_val, weight, (((1,), (1,)), ((), ())), preferred_ele...  54.5 us
    dot_general x6, matrix products, block_ssd(): y_part = jnp.einsum('ctsh,cshp->cthp', mix_w, x_groups, precision=HIGH)  37.6 us
    all_gather x2, blocking collectives, shards(): bc_all = lax.all_gather(bc_low, 'hd', axis=0, tiled=True)  32.6 us
  transfers between devices with their start and end apart: 24, of which 10 were waited for; matrix products, arithmetic and copies ran while one was open for 24% of the time, Pallas kernels for 0%

commit v1 on v0

--- a/solution.py
+++ b/solution.py
@@ -11,6 +11,24 @@
 DI = 3072
 HIGH = lax.Precision.HIGHEST
 EPS = 1e-05
+
+
+def ring_gather(shard, axis, dim):
+    ways, here, step = (lax.axis_size(axis), lax.axis_index(axis), shard.shape[dim])
+    lengths = [n * ways if d == dim else n for d, n in enumerate(shard.shape)]
+    full = lax.dynamic_update_slice_in_dim(
+        jnp.zeros(lengths, shard.dtype), shard, here * step, axis=dim
+    )
+    going_up = going_down = shard
+    for far in range(1, ways // 2 + 1):
+        going_up = lax.ppermute(going_up, axis, [(d, (d + 1) % ways) for d in range(ways)])
+        full = lax.dynamic_update_slice_in_dim(full, going_up, (here - far) % ways * step, axis=dim)
+        if 2 * far < ways:
+            going_down = lax.ppermute(going_down, axis, [(d, (d - 1) % ways) for d in range(ways)])
+            full = lax.dynamic_update_slice_in_dim(
+                full, going_down, (here + far) % ways * step, axis=dim
+            )
+    return full
 
 
 def from_behind(shard, axis, by):
@@ -195,7 +213,7 @@
             lax.all_to_all(x_low, "hd", split_axis=1, concat_axis=0, tiled=True),
             lax.all_to_all(rate_raw, "hd", split_axis=1, concat_axis=0, tiled=True),
         )
-        bc_all = lax.all_gather(bc_low, "hd", axis=0, tiled=True)
+        bc_all = ring_gather(bc_low, "hd", 0)
         x_float = x_heads.astype(jnp.float32)
         rate_float = rate_heads.astype(jnp.float32)
         bc_float = bc_all.astype(jnp.float32)

time: 1500 us -> 1450 us (0.967)
  blocking collectives: 177 us -> 145 us
  local copies, waits for them, and re-layouts: 179 us -> 159 us
    all_gather x2 -> x0, blocking collectives: 32.6 us -> none  [shards(): bc_all = lax.all_gather(bc_low, 'hd', axis=0, tiled=True)]
    another operation x26 -> x27, other arithmetic: 31.9 us -> 24.6 us
  transfers between devices with their start and end apart: 24 -> 30, of which waited for: 10 -> 13; matrix products, arithmetic and copies ran while one was open for 24% -> 26% of each run, Pallas kernels for 0% -> 0%
where the time goes in v1:
time: 1450 us; the launch traced here: 1430 us
  waiting for transfers between devices  686 us (47%)
  matrix products  220 us (15%)
  local copies, waits for them, and re-layouts  159 us (11%)
  blocking collectives  145 us (10%)
  other arithmetic  129 us (9%)
  starting transfers between devices  75.3 us (5%)
  between operations  17.3 us (1%)
    reduce_scatter x1, waiting for transfers between devices, shards(): lax.psum_scatter(lax.dot_general(part, proj_all, (((0,), (0,)), ((), ()))...  293 us
    reduce_scatter x1, waiting for transfers between devices, shards(): lax.psum_scatter(lax.dot_general(part, cot_all, (((0,), (0,)), ((), ())),...  215 us
    psum x1, waiting for transfers between devices, shards(): lax.psum((norm_total, taps_total, cbias_total, dtb_total, alog_total, ski...  125 us
    all_gather x1, blocking collectives, fetch(): lax.all_gather(dt_proj, ('dp', 'ctx', 'hd'), axis=0, tiled=True)  76.8 us
    all_gather x6, blocking collectives, carried_in(): lax.all_gather(part.astype(kind), axis)  68.4 us
    dot_general x8, matrix products, back_dot(): lax.dot_general(grad_val, weight, (((1,), (1,)), ((), ())), preferred_ele...  55.9 us
    dot_general x6, matrix products, block_ssd(): y_part = jnp.einsum('ctsh,cshp->cthp', mix_w, x_groups, precision=HIGH)  39.7 us
  transfers between devices with their start and end apart: 30, of which 13 were waited for; matrix products, arithmetic and copies ran while one was open for 26% of the time, Pallas kernels for 0%

profile of v1, /device:TPU:0, one launch (start us, length us, event | category | flops | bytes accessed | tf_op | source)
XLA Modules:
  0.0 1432.6 jit_solution(15815721886582029871)
XLA Ops:
  8.7 76.8 %all_gather.29 = bf16[1536,48]{1,0:T(8,128)(2,1)S(1)} all-gather(bf16[48,48]{1,0:T(8,128)(2,1)} %param.40), channel_id=1, replica_groups=mesh['dp'=2,'ctx'=4,'hd'=4] {'dp','ctx','hd'}, dimensions={0}, use_global_device_ids=true | all-gather | bytes 152064 | tf_op jit(solution)/shard_map/all_gather | solution.py:181
  104.7 5.0 all-to-all-start.1
  109.8 5.7 all-to-all-done.1
  126.1 14.2 all-gather.5
  143.4 6.4 all-gather.4
  151.0 6.8 convolution_convert_fusion
  172.2 6.0 collective-permute-start.1
  186.2 4.2 all-to-all-start.3
  209.1 4.8 all-to-all-start
  223.4 7.8 while.156
  232.2 13.3 all-gather.1
  245.6 7.1 while.157
  252.8 6.6 fusion.24
  262.7 3.6 reshape.750
  275.4 4.7 all-to-all-start.5
  289.6 7.8 while.154
  298.4 12.0 all-gather
  310.4 7.5 fusion.31
  317.9 7.0 while.155
  346.7 5.3 all-to-all-start.2
  353.6 6.2 while.152
  372.2 7.3 multiply_reduce_fusion.19
  380.1 9.3 multiply_reduce_fusion.13
  389.4 7.1 multiply_reduce_fusion.18
  396.6 9.1 multiply_convert_fusion.3
  405.7 5.0 multiply_convert_fusion.2
  413.0 4.2 all-to-all-start.9
  418.2 3.9 while.150
  424.4 8.8 all-to-all-done.9
  433.2 4.2 all-to-all-start.6
  445.9 10.8 all-gather.3
  470.2 7.8 while.153
  484.9 6.4 fusion.53
  499.8 11.6 all-gather.2
  511.5 4.4 while.158
  527.2 4.3 while.151
  536.8 6.4 fusion.51
  544.6 5.0 reduce-window.70
  554.0 5.0 reduce-window.76
  562.8 5.1 all-to-all-start.11
  568.5 5.0 all-to-all-done.11
  573.5 3.7 all-to-all-start.8
  577.2 6.5 fusion.116
  590.8 5.1 all-to-all-start.10
  595.8 6.4 fusion.109
  609.5 3.9 fusion.140
  617.5 5.2 all-to-all-start.7
  625.3 3.8 fusion.141
  630.9 4.0 fusion.139
  640.2 6.0 reduce-scatter.7.cloned.1.call-done
  646.3 4.2 multiply_reduce_fusion.5
  650.5 16.4 %reduce-scatter.5.cloned.1.call-done = bf16[128,256]{1,0:T(8,128)(2,1)} async-done(((bf16[512,256]{1,0:T(8,128)(2,1)}), bf16[128,256]{1,0:T(8,128)(2,1)}) %reduce-scatter.5.cloned.1.call-update) | async-done | bytes 65552 | tf_op jit(solution)/shard_map/reduce_scatter | solution.py:341
  667.0 5.9 multiply_reduce_fusion.9
  683.2 20.1 %fusion.38 = f32[1536,6448]{1,0:T(8,128)} fusion(bf16[128,48]{1,0:T(8,128)(2,1)S(1)} %copy.500, bf16[128,3328]{1,0:T(8,128)(2,1)S(1)} %fusion.98, bf16[128,3072]{1,0:T(8,128)(2,1)} %get-tuple-element.1177, bf16[128,48]{1,0:T(8,128)(2,1)S(1)} %copy.499, bf16[128,3328]{1,0:T(8,128)(2,1)S(1)} %fusion.99, bf16[128,3072]{1,0:T(8,128)(2,1)} %get-tuple-element.1175, ...), kind=kOutput, calls=%fused_computation.78 | convolution fusion | flops 5092294656 | bytes 43704320 | tf_op jit(solution)/shard_map/dot_general | solution.py:390
  706.0 7.9 fusion.276
  713.9 9.4 fusion.274
  730.4 9.3 convolution_add_fusion.2
  741.0 9.2 convolution_add_fusion.3
  752.4 11.7 fusion.118
  764.2 5.9 fusion.84
  770.1 5.2 fusion.85
  778.7 292.8 %reduce-scatter.9.cloned.1.call-done = f32[48,6448]{1,0:T(8,128)} async-done(((f32[1536,6448]{1,0:T(8,128)}), f32[48,6448]{1,0:T(8,128)}) %reduce-scatter.9.cloned.1.call-update) | async-done | bytes 1238032 | tf_op jit(solution)/shard_map/reduce_scatter | solution.py:389
  1076.7 125.0 %all-reduce.31.cloned.1.call-done = (f32[1536]{0:T(1024)}, f32[4,3328]{1,0:T(4,128)}, f32[3328]{0:T(1024)}, f32[48]{0:T(128)}, f32[48]{0:T(128)}, /*index=5*/f32[48]{0:T(128)}, f32[3072]{0:T(1024)}) async-done(((f32[1536]{0:T(1024)}, f32[4,3328]{1,0:T(4,128)}, f32[3328]{0:T(1024)}, f32[48]{0:T(128)}, f32[48]{0:T(128)}, /*index=5*/f32[48]{0:T(128)}, f32[3072]{0:T(1024)}), (f32[1536]{0:T(1024)}, ...) | async-done | bytes 85584 | tf_op jit(solution)/shard_map/psum | solution.py:406
  1201.7 214.8 %reduce-scatter.11.cloned.1.call-done = f32[96,1536]{1,0:T(8,128)} async-done(((f32[3072,1536]{1,0:T(8,128)}), f32[96,1536]{1,0:T(8,128)}) %reduce-scatter.11.cloned.1.call-update) | async-done | bytes 589840 | tf_op jit(solution)/shard_map/reduce_scatter | solution.py:398
  (789 shorter events, 342.4 us)
Async XLA Ops:
  7.2 79.9 %copy-start.12 = (bf16[2,128,1536]{2,1,0:T(8,128)(2,1)S(1)}, bf16[2,128,1536]{2,1,0:T(8,128)(2,1)}, u32[]{:S(2)}) copy-start(bf16[2,128,1536]{2,1,0:T(8,128)(2,1)} %param.35) | copy-start | bytes 2359300
  7.2 79.9 %copy-start.102 = (f32[1536]{0:T(1024)S(1)}, f32[1536]{0:T(1024)}, u32[]{:S(2)}) copy-start(f32[1536]{0:T(1024)} %param.37) | copy-start | bytes 18436
  7.2 143.8 %all-gather.10.cloned.1.call-start = ((), (), s32[]{:S(2)}) async-start(), calls=%async_computation.16 | async-start | bytes 10543104 | tf_op jit(solution)/shard_map/all_gather | solution.py:180
  7.9 364.2 %all-gather.12.cloned.1.call-start = ((), (), s32[]{:S(2)}) async-start(), calls=%async_computation.17 | async-start | bytes 9732096 | tf_op jit(solution)/shard_map/all_gather | solution.py:179
  87.6 63.4 %copy-start.18 = (bf16[128,1536]{1,0:T(8,128)(2,1)}, bf16[128,1536]{1,0:T(8,128)(2,1)S(1)}, u32[]{:S(2)}) copy-start(bf16[128,1536]{1,0:T(8,128)(2,1)S(1)} %get-tuple-element.1195) | copy-start | bytes 1179652
  87.6 72.4 %copy-start.15 = (bf16[128,1536]{1,0:T(8,128)(2,1)}, bf16[128,1536]{1,0:T(8,128)(2,1)S(1)}, u32[]{:S(2)}) copy-start(bf16[128,1536]{1,0:T(8,128)(2,1)S(1)} %get-tuple-element.1194) | copy-start | bytes 1179652
  87.6 15.7 %copy-start.151 = (f32[48]{0:T(128)S(1)}, f32[48]{0:T(128)}, u32[]{:S(2)}) copy-start(f32[48]{0:T(128)} %param.44) | copy-start | bytes 580
  87.9 15.5 %copy-start.159 = (f32[48]{0:T(128)S(1)}, f32[48]{0:T(128)}, u32[]{:S(2)}) copy-start(f32[48]{0:T(128)} %param.43) | copy-start | bytes 580
  87.9 16.2 %copy-start.160 = (f32[48]{0:T(128)S(1)}, f32[48]{0:T(128)}, u32[]{:S(2)}) copy-start(f32[48]{0:T(128)} %param.45) | copy-start | bytes 580
  88.5 16.2 %all-to-all-start.4 = ((bf16[128,4,12]{0,2,1:T(8,128)(2,1)}), bf16[128,4,12]{0,2,1:T(8,128)(2,1)S(1)}, u32[]{:S(2)}, u32[]{:S(2)}) async-start(bf16[128,4,12]{0,2,1:T(8,128)(2,1)} %all_to_all.141), calls=%async_computation.4 | async-start | bytes 32768 | tf_op jit(solution)/shard_map/all_to_all | solution.py:214
  91.8 288.2 %all-gather.14.cloned.1.call-start = ((), (), s32[]{:S(2)}) async-start(), calls=%async_computation.18 | async-start | bytes 9732096 | tf_op jit(solution)/shard_map/all_gather | solution.py:182
  98.6 69.6 %copy-start.71 = (f32[3328]{0:T(1024)}, f32[3328]{0:T(1024)S(1)}, u32[]{:S(2)}) copy-start(f32[3328]{0:T(1024)S(1)} %get-tuple-element.1033) | copy-start | bytes 39940
  101.9 21.7 %copy-start.98 = (f32[2,256]{1,0:T(2,128)}, f32[2,256]{1,0:T(2,128)S(1)}, u32[]{:S(2)}) copy-start(f32[2,256]{1,0:T(2,128)S(1)} %get-tuple-element.1242) | copy-start | bytes 6148
  101.9 21.7 %copy-start.114 = (f32[2,256]{1,0:T(2,128)}, f32[2,256]{1,0:T(2,128)S(1)}, u32[]{:S(2)}) copy-start(f32[2,256]{1,0:T(2,128)S(1)} %get-tuple-element.1243) | copy-start | bytes 6148
  101.9 21.7 %copy-start.113 = (f32[2,256]{1,0:T(2,128)}, f32[2,256]{1,0:T(2,128)S(1)}, u32[]{:S(2)}) copy-start(f32[2,256]{1,0:T(2,128)S(1)} %get-tuple-element.1249) | copy-start | bytes 6148
  103.4 15.8 %copy-start.133 = (f32[12]{0:T(128)}, f32[12]{0:T(128)S(1)}, u32[]{:S(2)}) copy-start(f32[12]{0:T(128)S(1)} %fusion.250) | copy-start | bytes 148
  103.5 20.1 %copy-start.134 = (f32[12]{0:T(128)}, f32[12]{0:T(128)S(1)}, u32[]{:S(2)}) copy-start(f32[12]{0:T(128)S(1)} %dynamic_slice.178) | copy-start | bytes 148
  104.7 10.8 all-to-all-start.1
  115.7 27.1 %copy-start.56 = (f32[2,256,12]{1,0,2:T(2,128)}, f32[2,256,12]{1,0,2:T(2,128)S(1)}, u32[]{:S(2)}) copy-start(f32[2,256,12]{1,0,2:T(2,128)S(1)} %reshape.754) | copy-start | bytes 73732
  115.8 27.0 %copy-start.54 = (f32[2,256,12]{1,0,2:T(2,128)}, f32[2,256,12]{1,0,2:T(2,128)S(1)}, u32[]{:S(2)}) copy-start(f32[2,256,12]{1,0,2:T(2,128)S(1)} %reshape.763) | copy-start | bytes 73732
  117.5 40.4 %copy-start.86 = (f32[2,12,256]{2,1,0:T(8,128)}, f32[2,12,256]{2,1,0:T(8,128)S(1)}, u32[]{:S(2)}) copy-start(f32[2,12,256]{2,1,0:T(8,128)S(1)} %reshape.833) | copy-start | bytes 73732
  120.9 37.0 %copy-start.52 = (f32[2,12,256]{2,1,0:T(8,128)}, f32[2,12,256]{2,1,0:T(8,128)S(1)}, u32[]{:S(2)}) copy-start(f32[2,12,256]{2,1,0:T(8,128)S(1)} %reshape.841) | copy-start | bytes 73732
  122.6 35.3 %copy-start.87 = (f32[2,12,256]{2,1,0:T(8,128)}, f32[2,12,256]{2,1,0:T(8,128)S(1)}, u32[]{:S(2)}) copy-start(f32[2,12,256]{2,1,0:T(8,128)S(1)} %reshape.835) | copy-start | bytes 73732
  123.6 34.3 %copy-start.79 = (f32[2,256,12]{1,2,0:T(8,128)}, f32[2,256,12]{1,2,0:T(8,128)S(1)}, u32[]{:S(2)}) copy-start(f32[2,256,12]{1,2,0:T(8,128)S(1)} %get-tuple-element.1225) | copy-start | bytes 73732
  123.6 34.3 %copy-start.84 = (f32[2,256,12]{1,2,0:T(8,128)}, f32[2,256,12]{1,2,0:T(8,128)S(1)}, u32[]{:S(2)}) copy-start(f32[2,256,12]{1,2,0:T(8,128)S(1)} %get-tuple-element.1271) | copy-start | bytes 73732
  125.9 32.0 %copy-start.65 = (f32[512,12]{0,1:T(8,128)}, f32[512,12]{0,1:T(8,128)S(1)}, u32[]{:S(2)}) copy-start(f32[512,12]{0,1:T(8,128)S(1)} %multiply_bitcast_fusion.2) | copy-start | bytes 73732
  158.0 5.6 collective-permute-start.4
  161.6 6.3 collective-permute-start
  167.1 25.6 %collective-permute-start.5 = (bf16[128,256]{1,0:T(8,128)(2,1)}, bf16[128,256]{1,0:T(8,128)(2,1)}, u32[]{:S(2)}, u32[]{:S(2)}) collective-permute-start(bf16[128,256]{1,0:T(8,128)(2,1)} %get-tuple-element.1192), channel_id=1, source_target_pairs={{0,1},{1,2},{2,3},{3,0},{4,5},{5,6},{6,7},{7,4},{8,9},{9,10},{10,1... | collective-permute-start | bytes 196616 | tf_op jit(solution)/shard_map/ppermute | solution.py:24
  172.2 22.5 %collective-permute-start.1 = (bf16[128,256]{1,0:T(8,128)(2,1)}, bf16[128,256]{1,0:T(8,128)(2,1)}, u32[]{:S(2)}, u32[]{:S(2)}) collective-permute-start(bf16[128,256]{1,0:T(8,128)(2,1)} %get-tuple-element.1190), channel_id=1, source_target_pairs={{0,1},{1,2},{2,3},{3,0},{4,5},{5,6},{6,7},{7,4},{8,9},{9,10},{10,1... | collective-permute-start | bytes 196616 | tf_op jit(solution)/shard_map/ppermute | solution.py:24
  178.9 20.3 %collective-permute-start.6 = (bf16[128,256]{1,0:T(8,128)(2,1)}, bf16[128,256]{1,0:T(8,128)(2,1)S(1)}, u32[]{:S(2)}, u32[]{:S(2)}) collective-permute-start(bf16[128,256]{1,0:T(8,128)(2,1)} %get-tuple-element.1192), channel_id=1, source_target_pairs={{0,3},{1,0},{2,1},{3,2},{4,7},{5,4},{6,5},{7,6},{8,11},{9,8},{10,9... | collective-permute-start | bytes 196616 | tf_op jit(solution)/shard_map/ppermute | solution.py:27
  180.9 18.9 %collective-permute-start.2 = (bf16[128,256]{1,0:T(8,128)(2,1)}, bf16[128,256]{1,0:T(8,128)(2,1)S(1)}, u32[]{:S(2)}, u32[]{:S(2)}) collective-permute-start(bf16[128,256]{1,0:T(8,128)(2,1)} %get-tuple-element.1190), channel_id=1, source_target_pairs={{0,3},{1,0},{2,1},{3,2},{4,7},{5,4},{6,5},{7,6},{8,11},{9,8},{10,9... | collective-permute-start | bytes 196616 | tf_op jit(solution)/shard_map/ppermute | solution.py:27
  186.2 22.9 %all-to-all-start.3 = ((bf16[128,4,768]{0,2,1:T(8,128)(2,1)}), bf16[128,4,768]{0,2,1:T(8,128)(2,1)}, u32[]{:S(2)}, u32[]{:S(2)}) async-start(bf16[128,4,768]{0,2,1:T(8,128)(2,1)} %bitcast.580), calls=%async_computation.3 | async-start | bytes 1572864 | tf_op jit(solution)/shard_map/all_to_all | solution.py:213
  192.7 10.8 collective-permute-start.7
  194.7 9.5 collective-permute-start.3
  209.1 66.3 %all-to-all-start = ((bf16[128,4,768]{0,2,1:T(8,128)(2,1)}), bf16[128,4,768]{0,2,1:T(8,128)(2,1)}, u32[]{:S(2)}, u32[]{:S(2)}) async-start(bf16[128,4,768]{0,2,1:T(8,128)(2,1)} %bitcast.579), calls=%async_computation | async-start | bytes 1572864 | tf_op jit(solution)/shard_map/all_to_all | solution.py:213
  275.4 71.3 %all-to-all-start.5 = ((bf16[4,128,768]{1,2,0:T(8,128)(2,1)}), bf16[4,128,768]{1,2,0:T(8,128)(2,1)}, u32[]{:S(2)}, u32[]{:S(2)}) async-start(bf16[4,128,768]{1,2,0:T(8,128)(2,1)} %copy.441), calls=%async_computation.5 | async-start | bytes 1572864 | tf_op jit(solution)/shard_map/all_to_all | solution.py:239
  346.7 20.0 %all-to-all-start.2 = ((bf16[4,128,768]{1,2,0:T(8,128)(2,1)}), bf16[4,128,768]{1,2,0:T(8,128)(2,1)}, u32[]{:S(2)}, u32[]{:S(2)}) async-start(bf16[4,128,768]{1,2,0:T(8,128)(2,1)} %copy.425), calls=%async_computation.2 | async-start | bytes 1572864 | tf_op jit(solution)/shard_map/all_to_all | solution.py:239
  380.0 16.5 %slice-start = ((s8[9437184]{0:T(1024)(128)(4,1)}), s8[4194304]{0:T(1024)(128)(4,1)S(1)}, s32[]{:S(2)}) async-start(s8[9437184]{0:T(1024)(128)(4,1)} %bitcast.551), calls=%async_computation.24 | async-start | bytes 8388608
  380.0 16.5 %slice-start.1 = ((s8[9437184]{0:T(1024)(128)(4,1)}), s8[4194304]{0:T(1024)(128)(4,1)S(1)}, s32[]{:S(2)}) async-start(s8[9437184]{0:T(1024)(128)(4,1)} %bitcast.551), calls=%async_computation.25 | async-start | bytes 8388608
  413.0 20.1 %all-to-all-start.9 = ((bf16[128,4,768]{0,2,1:T(8,128)(2,1)}), bf16[128,4,768]{0,2,1:T(8,128)(2,1)}, u32[]{:S(2)}, u32[]{:S(2)}) async-start(bf16[128,4,768]{0,2,1:T(8,128)(2,1)} %bitcast.581), calls=%async_computation.10 | async-start | bytes 1572864 | tf_op jit(solution)/shard_map/all_to_all | solution.py:300
  422.1 16.5 %copy-start.161 = (f32[2,12,1,1]{1,3,2,0:T(1,128)}, f32[2,12,1,1]{1,3,2,0:T(1,128)S(1)}, u32[]{:S(2)}) copy-start(f32[2,12,1,1]{1,3,2,0:T(1,128)S(1)} %get-tuple-element.1862) | copy-start | bytes 292
  433.2 58.1 %all-to-all-start.6 = ((bf16[128,4,768]{0,2,1:T(8,128)(2,1)}), bf16[128,4,768]{0,2,1:T(8,128)(2,1)}, u32[]{:S(2)}, u32[]{:S(2)}) async-start(bf16[128,4,768]{0,2,1:T(8,128)(2,1)} %bitcast.84), calls=%async_computation.6 | async-start | bytes 1572864 | tf_op jit(solution)/shard_map/all_to_all | solution.py:300
  536.8 16.3 %copy-start.88 = (f32[2,256,12]{1,2,0:T(8,128)S(1)}, f32[2,256,12]{1,2,0:T(8,128)}, u32[]{:S(2)}) copy-start(f32[2,256,12]{1,2,0:T(8,128)} %fusion.117) | copy-start | bytes 73732
  536.8 16.3 %copy-start.104 = (f32[2,256,12]{1,2,0:T(8,128)S(1)}, f32[2,256,12]{1,2,0:T(8,128)}, u32[]{:S(2)}) copy-start(f32[2,256,12]{1,2,0:T(8,128)} %get-tuple-element.1005) | copy-start | bytes 73732
  543.2 17.6 %copy-start.68 = (f32[2,8,4,128]{3,1,2,0:T(8,128)S(1)}, f32[2,8,4,128]{3,1,2,0:T(8,128)}, u32[]{:S(2)}) copy-start(f32[2,8,4,128]{3,1,2,0:T(8,128)} %copy-done.67) | copy-start | bytes 98308
  543.2 17.6 %copy-start.70 = (f32[2,8,4,128]{3,1,2,0:T(8,128)S(1)}, f32[2,8,4,128]{3,1,2,0:T(8,128)}, u32[]{:S(2)}) copy-start(f32[2,8,4,128]{3,1,2,0:T(8,128)} %copy-done.69) | copy-start | bytes 98308
  543.2 33.9 %copy-start.95 = (f32[2,256,12]{1,2,0:T(8,128)S(1)}, f32[2,256,12]{1,2,0:T(8,128)}, u32[]{:S(2)}) copy-start(f32[2,256,12]{1,2,0:T(8,128)} %get-tuple-element.1270) | copy-start | bytes 73732
  549.8 27.3 %copy-start.106 = (f32[2,256,12]{1,2,0:T(8,128)S(1)}, f32[2,256,12]{1,2,0:T(8,128)}, u32[]{:S(2)}) copy-start(f32[2,256,12]{1,2,0:T(8,128)} %copy-done.105) | copy-start | bytes 73732
  562.8 10.7 all-to-all-start.11
  573.5 17.3 %all-to-all-start.8 = ((bf16[4,128,12]{1,2,0:T(8,128)(2,1)}), bf16[4,128,12]{1,2,0:T(8,128)(2,1)S(1)}, u32[]{:S(2)}, u32[]{:S(2)}) async-start(bf16[4,128,12]{1,2,0:T(8,128)(2,1)} %copy.470), calls=%async_computation.9 | async-start | bytes 32768 | tf_op jit(solution)/shard_map/all_to_all | solution.py:337
  590.8 26.8 %all-to-all-start.10 = ((bf16[4,128,768]{1,2,0:T(8,128)(2,1)}), bf16[4,128,768]{1,2,0:T(8,128)(2,1)}, u32[]{:S(2)}, u32[]{:S(2)}) async-start(bf16[4,128,768]{1,2,0:T(8,128)(2,1)} %copy.484), calls=%async_computation.11 | async-start | bytes 1572864 | tf_op jit(solution)/shard_map/all_to_all | solution.py:334
  617.5 21.3 %all-to-all-start.7 = ((bf16[4,128,768]{1,2,0:T(8,128)(2,1)}), bf16[4,128,768]{1,2,0:T(8,128)(2,1)}, u32[]{:S(2)}, u32[]{:S(2)}) async-start(bf16[4,128,768]{1,2,0:T(8,128)(2,1)} %copy.456), calls=%async_computation.7 | async-start | bytes 1572864 | tf_op jit(solution)/shard_map/all_to_all | solution.py:334
  622.8 23.5 %reduce-scatter.7.cloned.1.call-start = ((), (), s32[]{:S(2)}) async-start(), calls=%async_computation.20 | async-start | bytes 327680 | tf_op jit(solution)/shard_map/reduce_scatter | solution.py:341
  625.0 41.9 %reduce-scatter.5.cloned.1.call-start = ((), (), s32[]{:S(2)}) async-start(), calls=%async_computation.19 | async-start | bytes 327680 | tf_op jit(solution)/shard_map/reduce_scatter | solution.py:341
  636.2 435.3 %reduce-scatter.9.cloned.1.call-start = ((), (), s32[]{:S(2)}) async-start(), calls=%async_computation.21 | async-start | bytes 41361408 | tf_op jit(solution)/shard_map/reduce_scatter | solution.py:389
  646.3 20.7 %copy-start.126 = (f32[128]{0:T(128)S(1)}, f32[128]{0:T(128)}, u32[]{:S(2)}) copy-start(f32[128]{0:T(128)} %get-tuple-element.1244) | copy-start | bytes 1540
  646.3 20.7 %copy-start.128 = (f32[128]{0:T(128)S(1)}, f32[128]{0:T(128)}, u32[]{:S(2)}) copy-start(f32[128]{0:T(128)} %get-tuple-element.1245) | copy-start | bytes 1540
  646.3 20.7 %copy-start.130 = (f32[128]{0:T(128)S(1)}, f32[128]{0:T(128)}, u32[]{:S(2)}) copy-start(f32[128]{0:T(128)} %get-tuple-element.1246) | copy-start | bytes 1540
  646.3 20.7 %copy-start.132 = (f32[128]{0:T(128)S(1)}, f32[128]{0:T(128)}, u32[]{:S(2)}) copy-start(f32[128]{0:T(128)} %get-tuple-element.1247) | copy-start | bytes 1540
  674.8 5.8 collective-permute-start.9
  676.7 6.4 collective-permute-start.8
  703.4 498.3 %all-reduce.31.cloned.1.call-start = ((), (), s32[]{:S(2)}) async-start(), calls=%async_computation.23 | async-start | bytes 183296 | tf_op jit(solution)/shard_map/psum | solution.py:406
  752.4 664.2 %reduce-scatter.11.cloned.1.call-start = ((), (), s32[]{:S(2)}) async-start(), calls=%async_computation.22 | async-start | bytes 19464192 | tf_op jit(solution)/shard_map/reduce_scatter | solution.py:398
  (135 other events, 681.0 us)
Sparse Core Ops, SparseCore 0:
  10.8 90.7 all-gather.9
  104.4 89.4 all-gather.11
  196.7 92.5 all-gather.13
  626.1 20.0 reduce-scatter.6
  649.0 17.8 reduce-scatter.4
  703.5 367.9 reduce-scatter.8
  1079.1 122.5 all-reduce.30
  1208.7 207.8 reduce-scatter.10
